TPU v7x, 256 devices: a whole 4x4x8 slice. The times are simulated.
256 devices in a mesh: row: 8 (over x, core), col: 16 (over y_lo, z), kern: 2 (over y_hi).
Axes of the slice: x: 4, y: 4 (y_hi: 2, y_lo: 2; y = y_hi * 2 + y_lo), z: 8, core: 2. Of those that a mesh axis runs over, the one named last changes fastest.
Arguments:
- mask_levels: int32 [256, 8192], P('row', 'col'), may hold values from 0 to 3
- level_offset: float32 [256, 8192], P('row', 'col'), may hold values from -6 to 6
- target_bits: int32 [256, 8192], P('row', 'col'), may hold values 0 or 1
- socs_kernels: bfloat16 [2, 24, 35, 35], P(None, 'kern'), may hold values from -0.067871094 to 0.067871094
- kernel_weights: float32 [24], P('kern'), may hold values from 0.1 to 1
Outputs:
- resist_image: float32 [256, 8192], P('row', 'col')
- mask_gradient: float32 [256, 8192], P('row', 'col')
All inputs are finite; a program needn't handle non-finite values. No bound on the sum of `target_bits` on one device may be relied on, other than what follows from the above.
Results may differ from a plain program's by a relative error of at most 0.0039.
Values may be sent and summed in bfloat16 or wider, within the bound.
No kernel may reach another device: no remote copies, remote signals or barrier semaphores. Data moves between devices by JAX's collectives and lax.ppermute only.
A program may use at most 64 MiB of HBM per device.

v0:
```python
import jax
import jax.numpy as jnp
from jax import lax
from jax.sharding import PartitionSpec as P

steepness = 4.0
threshold = 1.0
loss_gain = 32.0


def padded_2(value, sides, width):
    for axis, dim in sides:
        size, length = (lax.axis_size(axis), value.shape[dim])
        up = [(i, (i + 1) % size) for i in range(size - 1)]
        down = [(j, i) for i, j in up]
        last = lax.slice_in_dim(value, length - width, length, axis=dim)
        first = lax.slice_in_dim(value, 0, width, axis=dim)
        before = lax.ppermute(last, axis, up)
        after = lax.ppermute(first, axis, down)
        value = jnp.concatenate([before, value, after], axis=dim)
    return value


def column_windows(padded, blocks, reach):
    leading = padded.shape[:-1]
    central = padded[..., : blocks * 128].reshape(leading + (blocks, 128))
    filler = jnp.zeros(leading + (128 - reach,), padded.dtype)
    longer = jnp.concatenate([padded, filler], axis=-1)
    trailing = longer[..., 128:].reshape(leading + (blocks, 128))[..., :reach]
    return jnp.concatenate([central, trailing], axis=-1)


def band_select(stencil):
    window = 128 + stencil - 1
    offsets = (
        jnp.arange(window, dtype=jnp.int32)[:, None, None]
        - jnp.arange(128, dtype=jnp.int32)[None, :, None]
    )
    return (offsets == jnp.arange(stencil, dtype=jnp.int32)[None, None, :]).astype(jnp.bfloat16)


def forward_row(select, kernels, tap_row):
    kernel_row = lax.dynamic_index_in_dim(kernels, tap_row, 2, keepdims=False)
    toeplitz = jnp.einsum("job,ckb->jcko", select, kernel_row, preferred_element_type=jnp.float32)
    return toeplitz.astype(jnp.bfloat16).reshape(select.shape[0], -1)


def adjoint_row(select, flipped, tap_row):
    kernel_row = lax.dynamic_index_in_dim(flipped, tap_row, 2, keepdims=False)
    toeplitz = jnp.einsum("job,ckb->ckjo", select, kernel_row, preferred_element_type=jnp.float32)
    return toeplitz.astype(jnp.bfloat16).reshape(2 * flipped.shape[1], select.shape[0], 128)


def resist_terms(intensity, target):
    resist = jax.nn.sigmoid(steepness * (intensity - threshold))
    slope_term = (
        loss_gain * steepness * (resist - target.astype(jnp.float32)) * resist * (1.0 - resist)
    )
    return (resist, slope_term)


def per_device(mask_levels, level_offset, target_bits, socs_kernels, kernel_weights):
    tile_rows, tile_cols = mask_levels.shape
    stencil = socs_kernels.shape[-1]
    margin = stencil // 2
    reach = 2 * margin
    blocks = tile_cols // 128
    local_kernels = socs_kernels.shape[1]
    channels = 2 * local_kernels
    select = band_select(stencil)
    flipped = socs_kernels[:, :, ::-1, ::-1]
    mask_full = jax.nn.sigmoid(2.0 * (mask_levels.astype(jnp.float32) - 1.5) + level_offset)
    mask_bf = mask_full.astype(jnp.bfloat16)
    padded = padded_2(mask_bf, (("row", 0), ("col", 1)), margin)
    windows = column_windows(padded, blocks, reach)

    def forward_step(tap_row, running):
        row_slab = lax.dynamic_slice_in_dim(windows, tap_row, tile_rows, 0)
        weights_row = forward_row(select, socs_kernels, tap_row)
        return running + jnp.einsum(
            "xnj,jf->xnf", row_slab, weights_row, preferred_element_type=jnp.float32
        )

    fields = lax.fori_loop(
        0, stencil, forward_step, jnp.zeros((tile_rows, blocks, channels * 128), jnp.float32)
    )
    fields = fields.reshape(tile_rows, blocks, 2, local_kernels, 128)
    partial_value = jnp.sum(
        fields * fields * kernel_weights[None, None, None, :, None], axis=(2, 3)
    )
    partial_value = partial_value.reshape(tile_rows, tile_cols)
    intensity = lax.psum(partial_value, "kern")
    resist, slope_term = resist_terms(intensity, target_bits)
    scaled = (
        2.0
        * kernel_weights[None, None, None, :, None]
        * slope_term.reshape(tile_rows, blocks, 1, 1, 128)
    )
    charge = (scaled * fields).astype(jnp.bfloat16)
    charge = jnp.transpose(charge, (2, 3, 0, 1, 4)).reshape(channels, tile_rows, tile_cols)
    charge_padded = padded_2(charge, (("row", 1), ("col", 2)), margin)
    charge_windows = column_windows(charge_padded, blocks, reach)

    def adjoint_step(tap_row, running):
        row_slab = lax.dynamic_slice_in_dim(charge_windows, tap_row, tile_rows, 1)
        weights_row = adjoint_row(select, flipped, tap_row)
        return running + jnp.einsum(
            "cxnj,cjo->xno", row_slab, weights_row, preferred_element_type=jnp.float32
        )

    gradient_part = lax.fori_loop(
        0, stencil, adjoint_step, jnp.zeros((tile_rows, blocks, 128), jnp.float32)
    )
    gradient_part = gradient_part.reshape(tile_rows, tile_cols)
    summed = lax.psum(gradient_part, "kern")
    return (resist, summed * mask_full * (1.0 - mask_full))


def solution(mesh):
    return jax.shard_map(
        per_device,
        mesh=mesh,
        in_specs=(
            P("row", "col"),
            P("row", "col"),
            P("row", "col"),
            P(None, "kern", None, None),
            P("kern"),
        ),
        out_specs=(P("row", "col"), P("row", "col")),
        check_vma=False,
    )
```

profile of v0, /device:TPU:1, one launch (start us, length us, event | category | flops | bytes accessed | tf_op | source)
XLA Modules:
  0.0 472.6 jit_solution(10960512505497129558)
XLA Ops:
  8.1 4.5 collective-permute-start
  14.6 3.2 collective-permute-done.1
  17.9 3.5 collective-permute-start.2
  26.4 157.3 %while.28 = (s32[]{:T(128)}, f32[32,4,3072]{2,0,1:T(8,128)}, bf16[66,4,162]{2,0,1:T(8,128)(2,1)S(1)}, bf16[2,12,35,35]{3,1,0,2:T(8,128)(2,1)S(1)}, s32[162,128]{1,0:T(8,128)S(1)}, /*index=5*/s32[]{:T(128)}, s32[]{:T(128)}) while((s32[]{:T(128)}, f32[32,4,3072]{2,0,1:T(8,128)}, bf16[66,4,162]{2,0,1:T(8,128)(2,1)S(1)}, ...), condition=%wide.region_1.2_spmd.clone, body=%wide.region_0.1_spmd.clone.sunk | while | flops 164974080 | bytes 9314399 | solution.py:84
  62.8 3.0 convolution_add_fusion.2
  67.3 3.0 convolution_add_fusion.2
  71.8 3.0 convolution_add_fusion.2
  76.4 3.0 convolution_add_fusion.2
  80.9 3.0 convolution_add_fusion.2
  85.5 3.0 convolution_add_fusion.2
  90.0 3.0 convolution_add_fusion.2
  94.5 3.0 convolution_add_fusion.2
  99.1 3.0 convolution_add_fusion.2
  103.6 3.0 convolution_add_fusion.2
  108.1 3.0 convolution_add_fusion.2
  112.7 3.0 convolution_add_fusion.2
  117.2 3.0 convolution_add_fusion.2
  121.7 3.0 convolution_add_fusion.2
  126.3 3.0 convolution_add_fusion.2
  130.8 3.0 convolution_add_fusion.2
  135.3 3.0 convolution_add_fusion.2
  162.5 3.0 convolution_add_fusion.2
  186.8 36.1 %all-reduce.3.cloned.1.call-done = f32[32,512]{1,0:T(8,128)} async-done(((f32[32,512]{1,0:T(8,128)}), f32[32,512]{1,0:T(8,128)}) %all-reduce.3.cloned.1.call-update) | async-done | bytes 65552 | tf_op jit(solution)/shard_map/psum | solution.py:92
  226.4 4.1 collective-permute-start.4
  235.6 4.4 collective-permute-done.5
  241.1 3.2 collective-permute-start.6
  246.8 3.1 collective-permute-done.6
  253.5 6.0 %pad_maximum_fusion.4 = (bf16[24,66,512]{2,1,0:T(8,128)(2,1)S(1)}, bf16[24,66,512]{2,1,0:T(8,128)(2,1)}) fusion(bf16[24,66,17]{2,1,0:T(8,128)(2,1)} %copy-done.1, bf16[24,17,512]{2,1,0:T(8,128)(2,1)} %copy-done, bf16[24,32,512]{2,1,0:T(8,128)(2,1)S(1)} %reshape.72, bf16[24,17,512]{2,1,0:T(8,128)(2,1)S(1)} %copy.51, bf16[512]{0:T(512)(128)(2,1)S(1)} %pad_slice_fusion, ...), kind=kLoop, calls=%fused_computation.36 | loop fusion | flops 14598144 | bytes 4974784 | tf_op jit(solution)/shard_map/concatenate | solution.py:20
  259.5 3.7 reshape.86
  265.2 5.5 %pad_maximum_fusion = bf16[24,66,4,162]{3,2,1,0:T(4,128)(2,1)} fusion(bf16[24,66,4,34]{3,2,1,0:T(4,128)(2,1)} %bitcast.76, bf16[24,66,4,128]{3,2,1,0:T(4,128)(2,1)} %reshape.85), kind=kLoop, calls=%fused_computation.29 | loop fusion | flops 4105728 | bytes 4105728 | tf_op jit(solution)/shard_map/concatenate | solution.py:30
  270.8 155.4 %while.29 = (s32[]{:T(128)}, f32[32,4,128]{2,0,1:T(8,128)S(1)}, bf16[24,66,4,162]{3,2,1,0:T(4,128)(2,1)}, bf16[2,12,35,35]{3,1,0,2:T(8,128)(2,1)}, s32[162,128]{1,0:T(8,128)S(1)}, /*index=5*/s32[]{:T(128)}, s32[]{:T(128)}) while((s32[]{:T(128)}, f32[32,4,128]{2,0,1:T(8,128)S(1)}, bf16[24,66,4,162]{3,2,1,0:T(4,128)(2,1)}, ...), condition=%wide.region_5.6_spmd.clone, body=%wide.region_4.5_spmd.clone.sunk | while | flops 164220416 | bytes 7190107 | solution.py:111
  426.9 37.4 %all-reduce.5.cloned.1.call-done = f32[32,512]{1,0:T(8,128)} async-done(((f32[32,512]{1,0:T(8,128)}), f32[32,512]{1,0:T(8,128)}) %all-reduce.5.cloned.1.call-update) | async-done | bytes 65552 | tf_op jit(solution)/shard_map/psum | solution.py:115
  (322 shorter events, 286.9 us)
Async XLA Ops:
  7.2 215.7 %all-reduce.3.cloned.1.call-start = ((), (), s32[]{:S(2)}) async-start(), calls=%async_computation | async-start | bytes 131072 | tf_op jit(solution)/shard_map/psum | solution.py:92
  8.1 6.5 %collective-permute-start = (bf16[17,512]{1,0:T(8,128)(2,1)S(1)}, bf16[17,512]{1,0:T(8,128)(2,1)S(1)}, u32[]{:S(2)}, u32[]{:S(2)}) collective-permute-start(bf16[17,512]{1,0:T(8,128)(2,1)S(1)} %get-tuple-element.301), channel_id=1, source_target_pairs={{0,32},{32,64},{64,96},{96,128},{128,160},{160,192},{192,224},{1,3... | collective-permute-start | bytes 52232 | tf_op jit(solution)/shard_map/ppermute | solution.py:18
  12.7 5.1 %collective-permute-start.1 = (bf16[17,512]{1,0:T(8,128)(2,1)S(1)}, bf16[17,512]{1,0:T(8,128)(2,1)S(1)}, u32[]{:S(2)}, u32[]{:S(2)}) collective-permute-start(bf16[17,512]{1,0:T(8,128)(2,1)S(1)} %get-tuple-element.302), channel_id=1, source_target_pairs={{32,0},{64,32},{96,64},{128,96},{160,128},{192,160},{224,192},{33,... | collective-permute-start | bytes 52232 | tf_op jit(solution)/shard_map/ppermute | solution.py:19
  17.9 5.9 %collective-permute-start.2 = (bf16[66,17]{1,0:T(8,128)(2,1)S(1)}, bf16[66,17]{1,0:T(8,128)(2,1)S(1)}, u32[]{:S(2)}, u32[]{:S(2)}) collective-permute-start(bf16[66,17]{1,0:T(8,128)(2,1)S(1)} %get-tuple-element.299), channel_id=1, source_target_pairs={{0,2},{2,4},{4,6},{6,8},{8,10},{10,12},{12,14},{14,16},{16,18},{18... | collective-permute-start | bytes 6740 | tf_op jit(solution)/shard_map/ppermute | solution.py:18
  21.4 4.7 collective-permute-start.3
  183.7 1.7 copy-start.5
  185.4 37.5 %copy-start.4 = (s32[32,512]{1,0:T(8,128)S(1)}, s32[32,512]{1,0:T(8,128)}, u32[]{:S(2)}) copy-start(s32[32,512]{1,0:T(8,128)} %param.11) | copy-start | bytes 196612
  186.7 277.6 %all-reduce.5.cloned.1.call-start = ((), (), s32[]{:S(2)}) async-start(), calls=%async_computation.1 | async-start | bytes 131072 | tf_op jit(solution)/shard_map/psum | solution.py:115
  226.4 9.1 %collective-permute-start.4 = (bf16[24,17,512]{2,0,1:T(8,128)(2,1)S(1)}, bf16[24,17,512]{2,0,1:T(8,128)(2,1)S(1)}, u32[]{:S(2)}, u32[]{:S(2)}) collective-permute-start(bf16[24,17,512]{2,0,1:T(8,128)(2,1)S(1)} %copy.49), channel_id=1, source_target_pairs={{0,32},{32,64},{64,96},{96,128},{128,160},{160,192},{192,224},{1,3... | collective-permute-start | bytes 1253384 | tf_op jit(solution)/shard_map/ppermute | solution.py:18
  230.6 9.4 %collective-permute-start.5 = (bf16[24,17,512]{2,0,1:T(8,128)(2,1)S(1)}, bf16[24,17,512]{2,0,1:T(8,128)(2,1)S(1)}, u32[]{:S(2)}, u32[]{:S(2)}) collective-permute-start(bf16[24,17,512]{2,0,1:T(8,128)(2,1)S(1)} %copy.50), channel_id=1, source_target_pairs={{32,0},{64,32},{96,64},{128,96},{160,128},{192,160},{224,192},{33,... | collective-permute-start | bytes 1253384 | tf_op jit(solution)/shard_map/ppermute | solution.py:19
  240.1 9.8 %copy-start = (bf16[24,17,512]{2,1,0:T(8,128)(2,1)}, bf16[24,17,512]{2,1,0:T(8,128)(2,1)S(1)}, u32[]{:S(2)}) copy-start(bf16[24,17,512]{2,1,0:T(8,128)(2,1)S(1)} %copy.52) | copy-start | bytes 1253380
  241.1 8.7 %collective-permute-start.6 = (bf16[24,66,17]{2,1,0:T(8,128)(2,1)}, bf16[24,66,17]{2,1,0:T(8,128)(2,1)S(1)}, u32[]{:S(2)}, u32[]{:S(2)}) collective-permute-start(bf16[24,66,17]{2,1,0:T(8,128)(2,1)} %get-tuple-element.293), channel_id=1, source_target_pairs={{0,2},{2,4},{4,6},{6,8},{8,10},{10,12},{12,14},{14,16},{16,18},{18... | collective-permute-start | bytes 161576 | tf_op jit(solution)/shard_map/ppermute | solution.py:18
  244.3 9.2 %collective-permute-start.7 = (bf16[24,66,17]{2,1,0:T(8,128)(2,1)S(1)}, bf16[24,66,17]{2,1,0:T(8,128)(2,1)}, u32[]{:S(2)}, u32[]{:S(2)}) collective-permute-start(bf16[24,66,17]{2,1,0:T(8,128)(2,1)S(1)} %get-tuple-element.294), channel_id=1, source_target_pairs={{2,0},{4,2},{6,4},{8,6},{10,8},{12,10},{14,12},{16,14},{18,16},{20... | collective-permute-start | bytes 161576 | tf_op jit(solution)/shard_map/ppermute | solution.py:19
  249.9 0.8 copy-start.1
  270.8 193.5 %copy-start.2 = (f32[32,512]{1,0:T(8,128)S(1)}, f32[32,512]{1,0:T(8,128)}, u32[]{:S(2)}) copy-start(f32[32,512]{1,0:T(8,128)} %param.10) | copy-start | bytes 196612
  270.8 193.5 %copy-start.3 = (s32[32,512]{1,0:T(8,128)S(1)}, s32[32,512]{1,0:T(8,128)}, u32[]{:S(2)}) copy-start(s32[32,512]{1,0:T(8,128)} %param.9) | copy-start | bytes 196612
Sparse Core Ops, SparseCore 0:
  186.8 36.0 all-reduce.2
  427.0 37.2 all-reduce.4
where the time goes:
time: 477 us; the launch traced here: 473 us
  matrix products  192 us (40%)
  local copies, waits for them, and re-layouts  132 us (28%)
  waiting for transfers between devices  92.3 us (19%)
  starting transfers between devices  22 us (5%)
  other arithmetic  18 us (4%)
  between operations  14.3 us (3%)
    dot_general x35, matrix products, forward_step(): jnp.einsum('xnj,jf->xnf', row_slab, weights_row, preferred_element_type=j...  103 us
    dynamic_slice x35, local copies, waits for them, and re-layouts, adjoint_step(): row_slab = lax.dynamic_slice_in_dim(charge_windows, tap_row, tile_rows, 1)  77.8 us
    dot_general x35, matrix products, adjoint_row(): jnp.einsum('job,ckb->ckjo', select, kernel_row, preferred_element_type=jn...  46.3 us
    psum x1, waiting for transfers between devices, per_device(): summed = lax.psum(gradient_part, 'kern')  37.4 us
    psum x1, waiting for transfers between devices, per_device(): intensity = lax.psum(partial_value, 'kern')  36.1 us
    reshape x35, local copies, waits for them, and re-layouts, forward_row(): return toeplitz.astype(jnp.bfloat16).reshape(select.shape[0], -1)  23.3 us
    dot_general x35, matrix products, forward_row(): jnp.einsum('job,ckb->jcko', select, kernel_row, preferred_element_type=jn...  21.6 us
    dot_general x35, matrix products, adjoint_step(): jnp.einsum('cxnj,cjo->xno', row_slab, weights_row, preferred_element_type...  20.4 us
  transfers between devices with their start and end apart: 10, of which 8 were waited for; matrix products, arithmetic and copies ran while one was open for 0% of the time, Pallas kernels for 0%

commit v1 on v0

--- a/solution.py
+++ b/solution.py
@@ -112,7 +112,8 @@
         0, stencil, adjoint_step, jnp.zeros((tile_rows, blocks, 128), jnp.float32)
     )
     gradient_part = gradient_part.reshape(tile_rows, tile_cols)
-    summed = lax.psum(gradient_part, "kern")
+    open_the_masks = lambda m: jnp.sum(lax.all_gather(m, "kern"), axis=0)
+    summed = open_the_masks(gradient_part)
     return (resist, summed * mask_full * (1.0 - mask_full))
 
 

time: 477 us -> 449 us (0.941)
  the two profiles are of different devices: /device:TPU:1 before, /device:TPU:100 now
where the time goes in v1:
time: 449 us; the launch traced here: 445 us
  matrix products  192 us (43%)
  local copies, waits for them, and re-layouts  131 us (29%)
  waiting for transfers between devices  56.5 us (13%)
  starting transfers between devices  24.9 us (6%)
  other arithmetic  17.2 us (4%)
  between operations  14.3 us (3%)
  blocking collectives  6.45 us (1%)
    dot_general x35, matrix products, forward_step(): jnp.einsum('xnj,jf->xnf', row_slab, weights_row, preferred_element_type=j...  103 us
    dynamic_slice x35, local copies, waits for them, and re-layouts, adjoint_step(): row_slab = lax.dynamic_slice_in_dim(charge_windows, tap_row, tile_rows, 1)  77.8 us
    dot_general x35, matrix products, adjoint_row(): jnp.einsum('job,ckb->ckjo', select, kernel_row, preferred_element_type=jn...  46.3 us
    psum x1, waiting for transfers between devices, per_device(): intensity = lax.psum(partial_value, 'kern')  33.4 us
    reshape x35, local copies, waits for them, and re-layouts, forward_row(): return toeplitz.astype(jnp.bfloat16).reshape(select.shape[0], -1)  23.3 us
    dot_general x35, matrix products, forward_row(): jnp.einsum('job,ckb->jcko', select, kernel_row, preferred_element_type=jn...  21.6 us
    dot_general x35, matrix products, adjoint_step(): jnp.einsum('cxnj,cjo->xno', row_slab, weights_row, preferred_element_type...  20.4 us
    ppermute x4, starting transfers between devices, padded_2(): before = lax.ppermute(last, axis, up)  13.5 us
  transfers between devices with their start and end apart: 9, of which 7 were waited for; matrix products, arithmetic and copies ran while one was open for 1% of the time, Pallas kernels for 0%

profile of v1, /device:TPU:100, one launch (start us, length us, event | category | flops | bytes accessed | tf_op | source)
XLA Modules:
  0.0 444.8 jit_solution(4540591928133479722)
XLA Ops:
  10.1 3.6 collective-permute-start.1
  15.3 5.0 %collective-permute-start.2 = (bf16[66,17]{1,0:T(8,128)(2,1)S(1)}, bf16[66,17]{1,0:T(8,128)(2,1)S(1)}, u32[]{:S(2)}, u32[]{:S(2)}) collective-permute-start(bf16[66,17]{1,0:T(8,128)(2,1)S(1)} %get-tuple-element.299), channel_id=1, source_target_pairs={{0,2},{2,4},{4,6},{6,8},{8,10},{10,12},{12,14},{14,16},{16,18},{18... | collective-permute-start | bytes 6740 | tf_op jit(solution)/shard_map/ppermute | solution.py:18
  23.3 4.0 collective-permute-done.3
  27.6 157.3 %while.28 = (s32[]{:T(128)}, f32[32,4,3072]{2,0,1:T(8,128)}, bf16[66,4,162]{2,0,1:T(8,128)(2,1)S(1)}, bf16[2,12,35,35]{3,1,0,2:T(8,128)(2,1)S(1)}, s32[162,128]{1,0:T(8,128)S(1)}, /*index=5*/s32[]{:T(128)}, s32[]{:T(128)}) while((s32[]{:T(128)}, f32[32,4,3072]{2,0,1:T(8,128)}, bf16[66,4,162]{2,0,1:T(8,128)(2,1)S(1)}, ...), condition=%wide.region_1.2_spmd.clone, body=%wide.region_0.1_spmd.clone.sunk | while | flops 164974080 | bytes 9314399 | solution.py:84
  64.0 3.0 convolution_add_fusion.2
  68.5 3.0 convolution_add_fusion.2
  73.1 3.0 convolution_add_fusion.2
  77.6 3.0 convolution_add_fusion.2
  82.1 3.0 convolution_add_fusion.2
  86.7 3.0 convolution_add_fusion.2
  91.2 3.0 convolution_add_fusion.2
  95.7 3.0 convolution_add_fusion.2
  100.3 3.0 convolution_add_fusion.2
  104.8 3.0 convolution_add_fusion.2
  109.3 3.0 convolution_add_fusion.2
  113.9 3.0 convolution_add_fusion.2
  118.4 3.0 convolution_add_fusion.2
  122.9 3.0 convolution_add_fusion.2
  127.5 3.0 convolution_add_fusion.2
  132.0 3.0 convolution_add_fusion.2
  159.2 3.0 convolution_add_fusion.2
  187.9 33.4 %all-reduce.2.cloned.1.call-done = f32[32,512]{1,0:T(8,128)} async-done(((f32[32,512]{1,0:T(8,128)}), f32[32,512]{1,0:T(8,128)}) %all-reduce.2.cloned.1.call-update) | async-done | bytes 65552 | tf_op jit(solution)/shard_map/psum | solution.py:92
  226.9 3.6 collective-permute-start.5
  230.5 3.6 collective-permute-done.4
  237.3 4.7 %collective-permute-start.6 = (bf16[24,66,17]{2,1,0:T(8,128)(2,1)}, bf16[24,66,17]{2,1,0:T(8,128)(2,1)S(1)}, u32[]{:S(2)}, u32[]{:S(2)}) collective-permute-start(bf16[24,66,17]{2,1,0:T(8,128)(2,1)} %get-tuple-element.293), channel_id=1, source_target_pairs={{0,2},{2,4},{4,6},{6,8},{8,10},{10,12},{12,14},{14,16},{16,18},{18... | collective-permute-start | bytes 161576 | tf_op jit(solution)/shard_map/ppermute | solution.py:18
  245.0 7.4 %collective-permute-done.6 = bf16[24,66,17]{2,1,0:T(8,128)(2,1)S(1)} collective-permute-done((bf16[24,66,17]{2,1,0:T(8,128)(2,1)}, bf16[24,66,17]{2,1,0:T(8,128)(2,1)S(1)}, u32[]{:S(2)}, u32[]{:S(2)}) %collective-permute-start.6) | collective-permute-done | bytes 53888 | tf_op jit(solution)/shard_map/ppermute | solution.py:18
  253.1 4.8 %collective-permute-done.7 = bf16[24,66,17]{2,1,0:T(8,128)(2,1)} collective-permute-done((bf16[24,66,17]{2,1,0:T(8,128)(2,1)S(1)}, bf16[24,66,17]{2,1,0:T(8,128)(2,1)}, u32[]{:S(2)}, u32[]{:S(2)}) %collective-permute-start.7) | collective-permute-done | bytes 53888 | tf_op jit(solution)/shard_map/ppermute | solution.py:19
  258.0 6.0 %pad_maximum_fusion.4 = (bf16[24,66,512]{2,1,0:T(8,128)(2,1)S(1)}, bf16[24,66,512]{2,1,0:T(8,128)(2,1)}) fusion(bf16[24,66,17]{2,1,0:T(8,128)(2,1)} %copy-done.1, bf16[24,17,512]{2,1,0:T(8,128)(2,1)} %copy-done, bf16[24,32,512]{2,1,0:T(8,128)(2,1)S(1)} %reshape.69, bf16[24,17,512]{2,1,0:T(8,128)(2,1)S(1)} %copy.50, bf16[512]{0:T(512)(128)(2,1)S(1)} %pad_slice_fusion, ...), kind=kLoop, calls=%fused_computation.36 | loop fusion | flops 14598144 | bytes 4974784 | tf_op jit(solution)/shard_map/concatenate | solution.py:20
  264.0 3.7 reshape.82
  269.7 5.5 %pad_maximum_fusion = bf16[24,66,4,162]{3,2,1,0:T(4,128)(2,1)} fusion(bf16[24,66,4,34]{3,2,1,0:T(4,128)(2,1)} %bitcast.71, bf16[24,66,4,128]{3,2,1,0:T(4,128)(2,1)} %reshape.81), kind=kLoop, calls=%fused_computation.29 | loop fusion | flops 4105728 | bytes 4105728 | tf_op jit(solution)/shard_map/concatenate | solution.py:30
  275.2 155.4 %while.29 = (s32[]{:T(128)}, f32[32,4,128]{2,0,1:T(8,128)S(1)}, bf16[24,66,4,162]{3,2,1,0:T(4,128)(2,1)}, bf16[2,12,35,35]{3,1,0,2:T(8,128)(2,1)}, s32[162,128]{1,0:T(8,128)S(1)}, /*index=5*/s32[]{:T(128)}, s32[]{:T(128)}) while((s32[]{:T(128)}, f32[32,4,128]{2,0,1:T(8,128)S(1)}, bf16[24,66,4,162]{3,2,1,0:T(4,128)(2,1)}, ...), condition=%wide.region_5.6_spmd.clone, body=%wide.region_4.5_spmd.clone.sunk | while | flops 164220416 | bytes 7190107 | solution.py:111
  430.8 6.4 %all_gather.3 = f32[2,32,512]{2,1,0:T(8,128)S(1)} all-gather(f32[1,32,512]{2,1,0:T(8,128)S(1)} %all_gather_reshape.3), channel_id=1, replica_groups=mesh['row'=8,'col'=16,'kern'=2] {'kern'}, dimensions={0}, use_global_device_ids=true | all-gather | bytes 196608 | tf_op jit(solution)/shard_map/all_gather | solution.py:115
  (322 shorter events, 284.9 us)
Async XLA Ops:
  7.2 214.2 %all-reduce.2.cloned.1.call-start = ((), (), s32[]{:S(2)}) async-start(), calls=%async_computation | async-start | bytes 131072 | tf_op jit(solution)/shard_map/psum | solution.py:92
  8.1 5.6 %collective-permute-start = (bf16[17,512]{1,0:T(8,128)(2,1)S(1)}, bf16[17,512]{1,0:T(8,128)(2,1)S(1)}, u32[]{:S(2)}, u32[]{:S(2)}) collective-permute-start(bf16[17,512]{1,0:T(8,128)(2,1)S(1)} %get-tuple-element.301), channel_id=1, source_target_pairs={{0,32},{32,64},{64,96},{96,128},{128,160},{160,192},{192,224},{1,3... | collective-permute-start | bytes 52232 | tf_op jit(solution)/shard_map/ppermute | solution.py:18
  10.1 5.1 %collective-permute-start.1 = (bf16[17,512]{1,0:T(8,128)(2,1)S(1)}, bf16[17,512]{1,0:T(8,128)(2,1)S(1)}, u32[]{:S(2)}, u32[]{:S(2)}) collective-permute-start(bf16[17,512]{1,0:T(8,128)(2,1)S(1)} %get-tuple-element.302), channel_id=1, source_target_pairs={{32,0},{64,32},{96,64},{128,96},{160,128},{192,160},{224,192},{33,... | collective-permute-start | bytes 52232 | tf_op jit(solution)/shard_map/ppermute | solution.py:19
  15.3 8.0 %collective-permute-start.2 = (bf16[66,17]{1,0:T(8,128)(2,1)S(1)}, bf16[66,17]{1,0:T(8,128)(2,1)S(1)}, u32[]{:S(2)}, u32[]{:S(2)}) collective-permute-start(bf16[66,17]{1,0:T(8,128)(2,1)S(1)} %get-tuple-element.299), channel_id=1, source_target_pairs={{0,2},{2,4},{4,6},{6,8},{8,10},{10,12},{12,14},{14,16},{16,18},{18... | collective-permute-start | bytes 6740 | tf_op jit(solution)/shard_map/ppermute | solution.py:18
  20.3 7.0 %collective-permute-start.3 = (bf16[66,17]{1,0:T(8,128)(2,1)S(1)}, bf16[66,17]{1,0:T(8,128)(2,1)S(1)}, u32[]{:S(2)}, u32[]{:S(2)}) collective-permute-start(bf16[66,17]{1,0:T(8,128)(2,1)S(1)} %get-tuple-element.300), channel_id=1, source_target_pairs={{2,0},{4,2},{6,4},{8,6},{10,8},{12,10},{14,12},{16,14},{18,16},{20... | collective-permute-start | bytes 6740 | tf_op jit(solution)/shard_map/ppermute | solution.py:19
  184.9 1.7 copy-start.5
  186.6 34.7 %copy-start.4 = (s32[32,512]{1,0:T(8,128)S(1)}, s32[32,512]{1,0:T(8,128)}, u32[]{:S(2)}) copy-start(s32[32,512]{1,0:T(8,128)} %param.11) | copy-start | bytes 196612
  224.8 9.4 %collective-permute-start.4 = (bf16[24,17,512]{2,0,1:T(8,128)(2,1)S(1)}, bf16[24,17,512]{2,0,1:T(8,128)(2,1)S(1)}, u32[]{:S(2)}, u32[]{:S(2)}) collective-permute-start(bf16[24,17,512]{2,0,1:T(8,128)(2,1)S(1)} %copy.48), channel_id=1, source_target_pairs={{0,32},{32,64},{64,96},{96,128},{128,160},{160,192},{192,224},{1,3... | collective-permute-start | bytes 1253384 | tf_op jit(solution)/shard_map/ppermute | solution.py:18
  226.9 9.2 %collective-permute-start.5 = (bf16[24,17,512]{2,0,1:T(8,128)(2,1)S(1)}, bf16[24,17,512]{2,0,1:T(8,128)(2,1)S(1)}, u32[]{:S(2)}, u32[]{:S(2)}) collective-permute-start(bf16[24,17,512]{2,0,1:T(8,128)(2,1)S(1)} %copy.49), channel_id=1, source_target_pairs={{32,0},{64,32},{96,64},{128,96},{160,128},{192,160},{224,192},{33,... | collective-permute-start | bytes 1253384 | tf_op jit(solution)/shard_map/ppermute | solution.py:19
  236.2 16.2 %copy-start = (bf16[24,17,512]{2,1,0:T(8,128)(2,1)}, bf16[24,17,512]{2,1,0:T(8,128)(2,1)S(1)}, u32[]{:S(2)}) copy-start(bf16[24,17,512]{2,1,0:T(8,128)(2,1)S(1)} %copy.51) | copy-start | bytes 1253380
  237.3 15.1 %collective-permute-start.6 = (bf16[24,66,17]{2,1,0:T(8,128)(2,1)}, bf16[24,66,17]{2,1,0:T(8,128)(2,1)S(1)}, u32[]{:S(2)}, u32[]{:S(2)}) collective-permute-start(bf16[24,66,17]{2,1,0:T(8,128)(2,1)} %get-tuple-element.293), channel_id=1, source_target_pairs={{0,2},{2,4},{4,6},{6,8},{8,10},{10,12},{12,14},{14,16},{16,18},{18... | collective-permute-start | bytes 161576 | tf_op jit(solution)/shard_map/ppermute | solution.py:18
  241.9 16.1 %collective-permute-start.7 = (bf16[24,66,17]{2,1,0:T(8,128)(2,1)S(1)}, bf16[24,66,17]{2,1,0:T(8,128)(2,1)}, u32[]{:S(2)}, u32[]{:S(2)}) collective-permute-start(bf16[24,66,17]{2,1,0:T(8,128)(2,1)S(1)} %get-tuple-element.294), channel_id=1, source_target_pairs={{2,0},{4,2},{6,4},{8,6},{10,8},{12,10},{14,12},{16,14},{18,16},{20... | collective-permute-start | bytes 161576 | tf_op jit(solution)/shard_map/ppermute | solution.py:19
  252.4 0.8 copy-start.1
  275.2 162.0 %copy-start.2 = (f32[32,512]{1,0:T(8,128)S(1)}, f32[32,512]{1,0:T(8,128)}, u32[]{:S(2)}) copy-start(f32[32,512]{1,0:T(8,128)} %param.10) | copy-start | bytes 196612
  275.2 162.0 %copy-start.3 = (s32[32,512]{1,0:T(8,128)S(1)}, s32[32,512]{1,0:T(8,128)}, u32[]{:S(2)}) copy-start(s32[32,512]{1,0:T(8,128)} %param.9) | copy-start | bytes 196612
Sparse Core Ops, SparseCore 0:
  188.0 33.2 all-reduce.1
